TPU v7x, 512 devices: a whole 4x8x8 slice. The times are simulated.
512 devices in a mesh: segment: 2 (over core), dp: 64 (over y, z), rows: 4 (over x).
Axes of the slice: x: 4, y: 8, z: 8, core: 2. Of those that a mesh axis runs over, the one named last changes fastest.
Arguments:
- latent: bfloat16 [128, 16, 16, 320], P('dp', 'rows'), may hold values from -6 to 6
- hint: bfloat16 [128, 16, 16, 320], P('dp', 'rows'), may hold values from -6 to 6
- decoder_in: bfloat16 [128, 16, 16, 320], P('dp', 'rows'), may hold values from -6 to 6
- target: bfloat16 [128, 16, 16, 320], P('dp', 'rows'), may hold values from -6 to 6
- first_convs: bfloat16 [2, 2, 2880, 320], P('segment', None, 'dp'), may hold values from -0.109375 to 0.109375
- second_convs: bfloat16 [2, 2880, 320], P('segment', 'dp'), may hold values from -0.109375 to 0.109375
- pointwise_weights: bfloat16 [2, 2, 320, 320], P('segment', None, 'dp'), may hold values from -0.3125 to 0.3125
Outputs:
- grad_first: float32 [921600], P(('segment', 'dp', 'rows'))
- grad_zero: float32 [102400], P(('segment', 'dp', 'rows'))
All inputs are finite; a program needn't handle non-finite values.
Results may differ from a plain program's by a relative error of at most 0.0095.
Values may be sent and summed in bfloat16 or wider, within the bound.
A program may use at most 64 MiB of HBM per device.

v0:
```python
import math
import jax
import jax.numpy as jnp
from jax import lax
from jax.sharding import PartitionSpec as P


def padded_2(block, sides, width):
    for axis, dim in sides:
        count = lax.axis_size(axis)
        forward = [(i, i + 1) for i in range(count - 1)]
        backward = [(target, source) for source, target in forward]
        low = lax.ppermute(
            lax.slice_in_dim(block, block.shape[dim] - width, None, axis=dim), axis, forward
        )
        high = lax.ppermute(lax.slice_in_dim(block, 0, width, axis=dim), axis, backward)
        block = jnp.concatenate([low, block, high], axis=dim)
    return block


def shifted(array, axis, by):
    count = lax.axis_size(axis)
    pairs = [(i, i + by) for i in range(count) if 0 <= i + by < count]
    return lax.ppermute(array, axis, pairs)


def swish_slope(value):
    logistic = jax.nn.sigmoid(value)
    return logistic * (1.0 + value * (1.0 - logistic))


def conv_rows(padded, weight):
    kernel = weight.reshape(3, 3, weight.shape[0] // 9, weight.shape[1])
    return lax.conv_general_dilated(
        padded,
        kernel,
        (1, 1),
        ((0, 0), (1, 1)),
        dimension_numbers=("NHWC", "HWIO", "NHWC"),
        preferred_element_type=jnp.float32,
    )


def kernel_grad(padded, cotangent):
    result = lax.conv_general_dilated(
        padded,
        cotangent,
        (1, 1),
        ((0, 0), (1, 1)),
        dimension_numbers=("CHWN", "IHWO", "HWNC"),
        preferred_element_type=jnp.float32,
    )
    return result.reshape(-1, result.shape[-1])


def project(values, weight):
    flat = values.reshape(-1, values.shape[-1])
    return jnp.dot(flat, weight, preferred_element_type=jnp.float32).reshape(
        values.shape[:-1] + (weight.shape[1],)
    )


def flipped(weight, channels):
    grid = weight.reshape(3, 3, channels, channels)[::-1, ::-1]
    return jnp.swapaxes(grid, 2, 3).reshape(9 * channels, channels)


def contract_rows(left, right):
    return lax.dot_general(
        left, right, (((0,), (0,)), ((), ())), preferred_element_type=jnp.float32
    )


def per_device(latent, hint, decoder_in, target, first_convs, second_convs, pointwise_weights):
    samples, height, width, channels = latent.shape
    first_all, point_all = (
        lax.all_gather(first_convs, "dp", axis=2, tiled=True),
        lax.all_gather(pointwise_weights, "dp", axis=2, tiled=True),
    )
    second_all = lax.all_gather(second_convs, "dp", axis=1, tiled=True)
    first_left = first_all[0, 0]
    first_right = first_all[0, 1]
    second_main = second_all[0]
    second_back = flipped(second_main, channels)
    point_left = point_all[0, 0]
    point_right = point_all[0, 1]
    right_back = point_right.T
    segment_zero = lax.axis_index("segment") == 0
    scale = 1.0 / math.sqrt(samples * lax.axis_size("dp") * height * lax.axis_size("rows") * width)
    blocks = 1
    block = samples // blocks
    plane = (block, height, width, channels)
    empty = jnp.zeros(plane, jnp.bfloat16)
    received = jnp.zeros((2,) + plane, jnp.bfloat16)
    returned = empty
    error_half = empty
    dec_grad = empty
    grad_first = jnp.zeros((9 * channels, channels), jnp.float32)
    grad_zero = jnp.zeros((channels, channels), jnp.float32)
    saved = [None] * blocks
    for tick in range(blocks + 2):
        forward_zero = tick < blocks
        decode = 1 <= tick <= blocks
        backward_zero = tick >= 2
        if forward_zero or decode:
            first_index = min(tick, blocks - 1)

            def inputs_zero():
                mixed = (latent.astype(jnp.float32) + project(hint, point_left)).astype(
                    jnp.bfloat16
                )
                return jnp.stack([latent, mixed])

            def inputs_one():
                return jnp.stack([received[0], decoder_in])

            pair = lax.cond(segment_zero, inputs_zero, inputs_one)
            padded = padded_2(pair, (("rows", 2),), 1)
            out_left = conv_rows(padded[0], first_left)
            out_right = conv_rows(padded[1], first_right)

            def middle_zero():
                return jax.nn.silu(out_right).astype(jnp.bfloat16)

            def middle_one():
                return (
                    latent.astype(jnp.float32) + out_left + received[1].astype(jnp.float32)
                ).astype(jnp.bfloat16)

            middle = lax.cond(segment_zero, middle_zero, middle_one)
            padded_mid = padded_2(middle, (("rows", 1),), 1)
            out_mid = conv_rows(padded_mid, second_main)

            def finish_zero():
                enc_act = jax.nn.silu(out_left).astype(jnp.bfloat16)
                control_out = (pair[1].astype(jnp.float32) + out_mid).astype(jnp.bfloat16)
                control_proj = project(control_out, point_right).astype(jnp.bfloat16)
                return (jnp.stack([enc_act, control_proj]), control_out, empty, empty)

            def finish_one():
                dec_pre = out_right + out_mid
                output = (
                    jax.nn.silu(dec_pre)
                    + project(decoder_in, point_left)
                    + project(middle, point_right)
                )
                error = (output - target.astype(jnp.float32)) * scale
                return (
                    jnp.zeros((2,) + plane, jnp.bfloat16),
                    empty,
                    error.astype(jnp.bfloat16),
                    (error * swish_slope(dec_pre)).astype(jnp.bfloat16),
                )

            outgoing, control_out, error_half, dec_grad = lax.cond(
                segment_zero, finish_zero, finish_one
            )
            if forward_zero:
                saved[first_index] = (padded[1], out_right, control_out)
                received = shifted(outgoing, "segment", 1)
        if decode or backward_zero:
            incoming = returned

            def start_zero():
                return project(incoming, right_back).astype(jnp.bfloat16)

            def start_one():
                return dec_grad

            back = lax.cond(segment_zero, start_zero, start_one)
            padded_back = padded_2(back, (("rows", 1),), 1)
            out_back = conv_rows(padded_back, second_back)
            if backward_zero:
                held_input, held_pre, held_out = saved[tick - 2]

                def update_zero():
                    first_grad = (out_back * swish_slope(held_pre)).astype(jnp.bfloat16)
                    new_first = grad_first + kernel_grad(held_input, first_grad)
                    new_zero = grad_zero + contract_rows(
                        held_out.reshape(-1, channels), incoming.reshape(-1, channels)
                    )
                    return (new_first, new_zero, empty)

            else:

                def update_zero():
                    return (grad_first, grad_zero, empty)

            def update_one():
                skip_grad = (out_back + project(error_half, right_back)).astype(jnp.bfloat16)
                return (grad_first, grad_zero, skip_grad)

            grad_first, grad_zero, skip_grad = lax.cond(segment_zero, update_zero, update_one)
            if decode:
                returned = shifted(skip_grad, "segment", -1)
    flat_first = grad_first.reshape(-1)
    flat_zero = grad_zero.reshape(-1)
    out_first, out_zero = (
        lax.psum_scatter(flat_first, ("segment", "dp", "rows"), scatter_dimension=0, tiled=True),
        lax.psum_scatter(flat_zero, ("segment", "dp", "rows"), scatter_dimension=0, tiled=True),
    )
    return (out_first, out_zero)


def solution(mesh):
    placed = (
        P("dp", "rows", None, None),
        P("dp", "rows", None, None),
        P("dp", "rows", None, None),
        P("dp", "rows", None, None),
        P("segment", None, "dp", None),
        P("segment", "dp", None),
        P("segment", None, "dp", None),
    )
    return jax.shard_map(
        per_device,
        mesh=mesh,
        in_specs=placed,
        out_specs=(P(("segment", "dp", "rows")), P(("segment", "dp", "rows"))),
        check_vma=False,
    )
```

profile of v0, /device:TPU:17, one launch (start us, length us, event | category | flops | bytes accessed | tf_op | source)
XLA Modules:
  0.0 553.0 jit_solution(7433316878518394187)
XLA Ops:
  7.9 1.5 copy.145
  9.5 45.9 %all_gather.9 = bf16[1,2,320,320]{3,1,0,2:T(2,128)(2,1)S(1)} all-gather(bf16[1,2,5,320]{3,1,0,2:T(2,128)(2,1)} %bitcast.208), channel_id=1, replica_groups=mesh['segment'=2,'dp'=64,'rows'=4] {'dp'}, dimensions={2}, use_global_device_ids=true | all-gather | bytes 416000 | tf_op jit(solution)/shard_map/all_gather | solution.py:78
  56.3 3.1 collective-permute-start
  59.4 1.3 collective-permute-start.1
  61.0 3.2 collective-permute-done.1
  65.7 32.6 %all-gather.3.cloned.1.call-done = bf16[1,2,2880,320]{3,1,0,2:T(2,128)(2,1)} async-done(((bf16[1,2,45,320]{3,1,0,2:T(2,128)(2,1)}), bf16[1,2,2880,320]{3,1,0,2:T(2,128)(2,1)}) %all-gather.3.cloned.1.call-update) | async-done | bytes 3686416 | tf_op jit(solution)/shard_map/all_gather | solution.py:77
  98.3 9.5 %fusion.71 = (bf16[1,1,2880,320]{3,1,0,2:T(2,128)(2,1)S(1)}, bf16[1,1,2880,320]{3,1,0,2:T(2,128)(2,1)S(1)}) fusion(bf16[1,2,2880,320]{3,1,0,2:T(2,128)(2,1)} %all-gather.3.cloned.1.call-done), kind=kLoop, calls=%fused_computation.126 | loop fusion | bytes 7372800 | tf_op jit(solution)/shard_map/slice | solution.py:81
  114.3 4.6 collective-permute-start.2
  118.9 66.2 %all-gather.5.cloned.1.call-done = bf16[1,2880,320]{2,0,1:T(2,128)(2,1)} async-done(((bf16[1,45,320]{2,0,1:T(2,128)(2,1)}), bf16[1,2880,320]{2,0,1:T(2,128)(2,1)}) %all-gather.5.cloned.1.call-update) | async-done | bytes 1843216 | tf_op jit(solution)/shard_map/all_gather | solution.py:80
  185.1 2.6 copy.189
  192.2 7.1 %collective-permute-done.4 = bf16[2,2,4,16,320]{4,3,2,1,0:T(8,128)(2,1)} collective-permute-done((bf16[2,2,4,16,320]{4,3,2,1,0:T(8,128)(2,1)S(1)}, bf16[2,2,4,16,320]{4,3,2,1,0:T(8,128)(2,1)}, u32[]{:S(2)}, u32[]{:S(2)}) %collective-permute-start.4) | collective-permute-done | bytes 163872 | tf_op jit(solution)/shard_map/ppermute | solution.py:24
  200.3 1.4 collective-permute-start.6
  201.7 4.2 collective-permute-start.5
  212.0 1.3 collective-permute-start.8
  213.3 4.3 collective-permute-start.7
  222.0 4.3 collective-permute-start.9
  229.4 4.4 collective-permute-start.11
  236.1 4.6 collective-permute-start.12
  243.5 2.4 conditional.25
  243.5 2.3 broadcast_in_dim.13
  245.9 5.7 %reshape.49 = f32[921600]{0:T(1024)} reshape(f32[2880,320]{1,0:T(8,128)} %get-tuple-element.146) | data formatting | bytes 7372800 | tf_op jit(solution)/shard_map/reshape | solution.py:196
  252.7 291.1 %all-reduce.6.cloned.1.call-done = (f32[921600]{0:T(1024)}, f32[102400]{0:T(1024)}) async-done(((f32[921600]{0:T(1024)}, f32[102400]{0:T(1024)}), (f32[921600]{0:T(1024)}, f32[102400]{0:T(1024)})) %all-reduce.6.cloned.1.call-update) | async-done | bytes 4096016
  543.8 1.4 dynamic-slice
  545.2 1.3 dynamic-slice.1
  (144 shorter events, 37.8 us)
Async XLA Ops:
  7.2 91.1 %all-gather.3.cloned.1.call-start = ((), (), s32[]{:S(2)}) async-start(), calls=%async_computation | async-start | bytes 4492800 | tf_op jit(solution)/shard_map/all_gather | solution.py:77
  7.2 48.9 %copy-start = (bf16[2,4,16,320]{3,2,1,0:T(8,128)(2,1)S(1)}, bf16[2,4,16,320]{3,2,1,0:T(8,128)(2,1)}, u32[]{:S(2)}) copy-start(bf16[2,4,16,320]{3,2,1,0:T(8,128)(2,1)} %param.27) | copy-start | bytes 245764
  7.2 48.9 %copy-start.5 = (bf16[2,4,16,320]{3,2,1,0:T(8,128)(2,1)S(1)}, bf16[2,4,16,320]{3,2,1,0:T(8,128)(2,1)}, u32[]{:S(2)}) copy-start(bf16[2,4,16,320]{3,2,1,0:T(8,128)(2,1)} %param.29) | copy-start | bytes 245764
  7.2 48.9 %copy-start.8 = (bf16[2,4,16,320]{3,2,1,0:T(8,128)(2,1)S(1)}, bf16[2,4,16,320]{3,2,1,0:T(8,128)(2,1)}, u32[]{:S(2)}) copy-start(bf16[2,4,16,320]{3,2,1,0:T(8,128)(2,1)} %param.28) | copy-start | bytes 245764
  7.9 177.2 %all-gather.5.cloned.1.call-start = ((), (), s32[]{:S(2)}) async-start(), calls=%async_computation.1 | async-start | bytes 4492800 | tf_op jit(solution)/shard_map/all_gather | solution.py:80
  9.4 534.3 %all-reduce.6.cloned.1.call-start = ((), (), s32[]{:S(2)}) async-start(), calls=%async_computation.2 | async-start | bytes 8192000
  56.3 4.5 collective-permute-start
  59.4 4.8 collective-permute-start.1
  110.0 1.4 copy-start.1
  113.0 74.7 %collective-permute-start.3 = (bf16[2,1,16,320]{3,2,1,0:T(8,128)(2,1)}, bf16[2,1,16,320]{3,2,1,0:T(8,128)(2,1)}, u32[]{:S(2)}, u32[]{:S(2)}) collective-permute-start(bf16[2,1,16,320]{3,2,1,0:T(8,128)(2,1)} %get-tuple-element.279), channel_id=1, source_target_pairs={{1,0},{2,1},{3,2},{5,4},{6,5},{7,6},{9,8},{10,9},{11,10},{13,12},{... | collective-permute-start | bytes 61448 | tf_op jit(solution)/shard_map/ppermute | solution.py:16
  114.3 73.4 %collective-permute-start.2 = (bf16[2,1,16,320]{3,2,1,0:T(8,128)(2,1)}, bf16[2,1,16,320]{3,2,1,0:T(8,128)(2,1)}, u32[]{:S(2)}, u32[]{:S(2)}) collective-permute-start(bf16[2,1,16,320]{3,2,1,0:T(8,128)(2,1)} %get-tuple-element.278), channel_id=1, source_target_pairs={{0,1},{1,2},{2,3},{4,5},{5,6},{6,7},{8,9},{9,10},{10,11},{12,13},{... | collective-permute-start | bytes 61448 | tf_op jit(solution)/shard_map/ppermute | solution.py:13
  190.0 9.3 %copy-start.6 = (bf16[2,4,16,320]{3,2,1,0:T(8,128)(2,1)S(1)}, bf16[2,4,16,320]{3,2,1,0:T(8,128)(2,1)}, u32[]{:S(2)}) copy-start(bf16[2,4,16,320]{3,2,1,0:T(8,128)(2,1)} %param.29) | copy-start | bytes 245764
  190.9 8.4 %collective-permute-start.4 = (bf16[2,2,4,16,320]{4,3,2,1,0:T(8,128)(2,1)S(1)}, bf16[2,2,4,16,320]{4,3,2,1,0:T(8,128)(2,1)}, u32[]{:S(2)}, u32[]{:S(2)}) collective-permute-start(bf16[2,2,4,16,320]{4,3,2,1,0:T(8,128)(2,1)S(1)} %get-tuple-element.142), channel_id=1, source_target_pairs={{0,256},{1,257},{2,258},{3,259},{4,260},{5,261},{6,262},{7,263},{8... | collective-permute-start | bytes 491528 | tf_op jit(solution)/shard_map/ppermute | solution.py:24
  200.2 7.5 %copy-start.4 = (bf16[1,1,2880,320]{3,2,1,0:T(8,128)(2,1)S(1)}, bf16[1,1,2880,320]{3,2,1,0:T(8,128)(2,1)}, u32[]{:S(2)}) copy-start(bf16[1,1,2880,320]{3,2,1,0:T(8,128)(2,1)} %copy-done.3) | copy-start | bytes 5529604
  200.3 5.6 %collective-permute-start.6 = (bf16[2,2,1,16,320]{4,3,2,1,0:T(8,128)(2,1)S(1)}, bf16[2,2,1,16,320]{4,3,2,1,0:T(8,128)(2,1)S(1)}, u32[]{:S(2)}, u32[]{:S(2)}) collective-permute-start(bf16[2,2,1,16,320]{4,3,2,1,0:T(8,128)(2,1)S(1)} %get-tuple-element.269), channel_id=1, source_target_pairs={{1,0},{2,1},{3,2},{5,4},{6,5},{7,6},{9,8},{10,9},{11,10},{13,12},{... | collective-permute-start | bytes 122888 | tf_op jit(solution)/shard_map/ppermute | solution.py:16
  201.7 5.2 collective-permute-start.5
  208.5 1.6 copy-start.2
  212.0 5.6 %collective-permute-start.8 = (bf16[2,1,16,320]{3,2,1,0:T(8,128)(2,1)S(1)}, bf16[2,1,16,320]{3,2,1,0:T(8,128)(2,1)S(1)}, u32[]{:S(2)}, u32[]{:S(2)}) collective-permute-start(bf16[2,1,16,320]{3,2,1,0:T(8,128)(2,1)S(1)} %get-tuple-element.277), channel_id=1, source_target_pairs={{1,0},{2,1},{3,2},{5,4},{6,5},{7,6},{9,8},{10,9},{11,10},{13,12},{... | collective-permute-start | bytes 61448 | tf_op jit(solution)/shard_map/ppermute | solution.py:16
  213.3 5.2 collective-permute-start.7
  220.7 5.6 %collective-permute-start.10 = (bf16[2,1,16,320]{3,2,1,0:T(8,128)(2,1)S(1)}, bf16[2,1,16,320]{3,2,1,0:T(8,128)(2,1)S(1)}, u32[]{:S(2)}, u32[]{:S(2)}) collective-permute-start(bf16[2,1,16,320]{3,2,1,0:T(8,128)(2,1)S(1)} %get-tuple-element.275), channel_id=1, source_target_pairs={{1,0},{2,1},{3,2},{5,4},{6,5},{7,6},{9,8},{10,9},{11,10},{13,12},{... | collective-permute-start | bytes 61448 | tf_op jit(solution)/shard_map/ppermute | solution.py:16
  222.0 5.2 collective-permute-start.9
  229.4 5.3 collective-permute-start.11
  234.8 5.9 %collective-permute-start.13 = (bf16[2,1,16,320]{3,2,1,0:T(8,128)(2,1)S(1)}, bf16[2,1,16,320]{3,2,1,0:T(8,128)(2,1)S(1)}, u32[]{:S(2)}, u32[]{:S(2)}) collective-permute-start(bf16[2,1,16,320]{3,2,1,0:T(8,128)(2,1)S(1)} %get-tuple-element.273), channel_id=1, source_target_pairs={{1,0},{2,1},{3,2},{5,4},{6,5},{7,6},{9,8},{10,9},{11,10},{13,12},{... | collective-permute-start | bytes 61448 | tf_op jit(solution)/shard_map/ppermute | solution.py:16
  236.1 5.5 collective-permute-start.12
  (5 other events, 5.1 us)
Sparse Core Ops, SparseCore 0:
  11.0 87.2 all-gather.2
  101.4 83.6 all-gather.4
  252.8 290.8 all-reduce.5
where the time goes:
time: 554 us; the launch traced here: 553 us
  waiting for transfers between devices  406 us (73%)
  blocking collectives  45.9 us (8%)
  starting transfers between devices  38.6 us (7%)
  local copies, waits for them, and re-layouts  37 us (7%)
  between operations  14.7 us (3%)
  matrix products  7.18 us (1%)
    unnamed x4, waiting for transfers between devices  292 us
    all_gather x1, waiting for transfers between devices, per_device(): second_all = lax.all_gather(second_convs, 'dp', axis=1, tiled=True)  66.2 us
    all_gather x1, blocking collectives, per_device(): lax.all_gather(pointwise_weights, 'dp', axis=2, tiled=True)  45.9 us
    all_gather x1, waiting for transfers between devices, per_device(): lax.all_gather(first_convs, 'dp', axis=2, tiled=True)  32.6 us
    ppermute x6, starting transfers between devices, padded_2(): lax.ppermute(lax.slice_in_dim(block, block.shape[dim] - width, None, axis...  25 us
  transfers between devices with their start and end apart: 17, of which 10 were waited for; matrix products, arithmetic and copies ran while one was open for 4% of the time, Pallas kernels for 0%

commit v1 on v0

--- a/solution.py
+++ b/solution.py
@@ -3,6 +3,13 @@
 import jax.numpy as jnp
 from jax import lax
 from jax.sharding import PartitionSpec as P
+
+track_sample = lambda content, a_name: jnp.concatenate(
+    lax.all_to_all(
+        jnp.stack(lax.axis_size(a_name) * [content]), axis_name=a_name, split_axis=0, concat_axis=0
+    ),
+    axis=2,
+)
 
 
 def padded_2(block, sides, width):
@@ -74,7 +81,7 @@
 def per_device(latent, hint, decoder_in, target, first_convs, second_convs, pointwise_weights):
     samples, height, width, channels = latent.shape
     first_all, point_all = (
-        lax.all_gather(first_convs, "dp", axis=2, tiled=True),
+        track_sample(first_convs, "dp"),
         lax.all_gather(pointwise_weights, "dp", axis=2, tiled=True),
     )
     second_all = lax.all_gather(second_convs, "dp", axis=1, tiled=True)

time: 554 us -> 606 us (1.094)
  blocking collectives: 45.9 us -> 165 us
  waiting for transfers between devices: 406 us -> 318 us
  starting transfers between devices: 38.6 us -> 53.2 us
    all_gather x1, blocking collectives: 45.9 us -> 165 us  [per_device(): lax.all_gather(pointwise_weights, 'dp', axis=2, tiled=True)]
    all_gather x1, waiting for transfers between devices: 66.2 us -> 0.01 us  [per_device(): second_all = lax.all_gather(second_convs, 'dp', axis=1, tiled=True)]
    all_gather x1 -> x0, waiting for transfers between devices: 32.6 us -> none  [per_device(): lax.all_gather(first_convs, 'dp', axis=2, tiled=True)]
    all_to_all x0 -> x1, starting transfers between devices: none -> 16.2 us  [lax.all_to_all(jnp.stack(lax.axis_size(a_name) * [content]), axis_name=a_...]
    ppermute x2, waiting for transfers between devices: 8.03 us -> 17.1 us  [shifted(): return lax.ppermute(array, axis, pairs)]
    unnamed x4 -> x3, waiting for transfers between devices: 292 us -> 293 us
  transfers between devices with their start and end apart: 17 -> 17, of which waited for: 10 -> 8; matrix products, arithmetic and copies ran while one was open for 4% -> 3% of each run, Pallas kernels for 0% -> 0%
where the time goes in v1:
time: 606 us; the launch traced here: 604 us
  waiting for transfers between devices  318 us (52%)
  blocking collectives  165 us (27%)
  starting transfers between devices  53.2 us (9%)
  local copies, waits for them, and re-layouts  41.7 us (7%)
  between operations  15 us (2%)
  matrix products  7.18 us (1%)
    unnamed x3, waiting for transfers between devices  293 us
    all_gather x1, blocking collectives, per_device(): lax.all_gather(pointwise_weights, 'dp', axis=2, tiled=True)  165 us
    ppermute x6, starting transfers between devices, padded_2(): lax.ppermute(lax.slice_in_dim(block, block.shape[dim] - width, None, axis...  23.4 us
    ppermute x2, waiting for transfers between devices, shifted(): return lax.ppermute(array, axis, pairs)  17.1 us
    all_to_all x1, starting transfers between devices, lax.all_to_all(jnp.stack(lax.axis_size(a_name) * [content]), axis_name=a_...  16.2 us
  transfers between devices with their start and end apart: 17, of which 8 were waited for; matrix products, arithmetic and copies ran while one was open for 3% of the time, Pallas kernels for 0%

profile of v1, /device:TPU:17, one launch (start us, length us, event | category | flops | bytes accessed | tf_op | source)
XLA Modules:
  0.0 604.4 jit_solution(11828064351746311758)
XLA Ops:
  7.2 5.3 stack.28
  12.5 16.2 %all-to-all-start = ((bf16[64,1,2,45,320]{4,2,3,1,0:T(2,128)(2,1)}), bf16[64,1,2,45,320]{4,2,3,1,0:T(2,128)(2,1)}, u32[]{:S(2)}, u32[]{:S(2)}) async-start(bf16[64,1,2,45,320]{4,2,3,1,0:T(2,128)(2,1)} %stack.28), calls=%async_computation | async-start | bytes 8847360 | tf_op jit(solution)/shard_map/all_to_all | solution.py:8
  29.6 165.4 %all_gather.6 = bf16[1,2,320,320]{3,1,0,2:T(2,128)(2,1)S(1)} all-gather(bf16[1,2,5,320]{3,1,0,2:T(2,128)(2,1)S(1)} %bitcast.211), channel_id=1, replica_groups=mesh['segment'=2,'dp'=64,'rows'=4] {'dp'}, dimensions={2}, use_global_device_ids=true | all-gather | bytes 416000 | tf_op jit(solution)/shard_map/all_gather | solution.py:85
  195.9 1.4 collective-permute-start
  197.4 1.3 collective-permute-start.1
  199.0 3.6 collective-permute-done.1
  204.1 9.5 %fusion.71 = (bf16[1,1,2880,320]{3,1,2,0:T(2,128)(2,1)S(1)}, bf16[1,1,2880,320]{3,1,2,0:T(2,128)(2,1)S(1)}) fusion(bf16[1,2,2880,320]{3,1,2,0:T(2,128)(2,1)} %bitcast.35), kind=kLoop, calls=%fused_computation.126 | loop fusion | bytes 7372800 | tf_op jit(solution)/shard_map/slice | solution.py:88
  220.1 4.6 collective-permute-start.2
  224.7 2.6 copy.229
  231.8 16.2 %collective-permute-done.4 = bf16[2,2,4,16,320]{4,3,2,1,0:T(8,128)(2,1)} collective-permute-done((bf16[2,2,4,16,320]{4,3,2,1,0:T(8,128)(2,1)S(1)}, bf16[2,2,4,16,320]{4,3,2,1,0:T(8,128)(2,1)}, u32[]{:S(2)}, u32[]{:S(2)}) %collective-permute-start.4) | collective-permute-done | bytes 163872 | tf_op jit(solution)/shard_map/ppermute | solution.py:31
  249.0 1.4 collective-permute-start.6
  250.4 4.0 collective-permute-start.5
  260.7 1.3 collective-permute-start.8
  262.0 4.3 collective-permute-start.7
  269.5 1.3 collective-permute-start.10
  270.8 4.3 collective-permute-start.9
  278.2 4.4 collective-permute-start.11
  284.8 4.8 collective-permute-start.12
  292.3 2.4 conditional.25
  292.3 2.4 broadcast_in_dim.13
  294.7 5.7 reshape.60
  301.5 293.4 %all-reduce.6.cloned.1.call-done = (f32[921600]{0:T(1024)}, f32[102400]{0:T(1024)}) async-done(((f32[921600]{0:T(1024)}, f32[102400]{0:T(1024)}), (f32[921600]{0:T(1024)}, f32[102400]{0:T(1024)})) %all-reduce.6.cloned.1.call-update) | async-done | bytes 4096016
  594.9 1.4 dynamic-slice
  596.3 1.3 dynamic-slice.1
  (152 shorter events, 36.5 us)
Async XLA Ops:
  12.5 16.3 %copy-start.12 = (bf16[1,45,320]{2,1,0:T(8,128)(2,1)S(1)}, bf16[1,45,320]{2,1,0:T(8,128)(2,1)}, u32[]{:S(2)}) copy-start(bf16[1,45,320]{2,1,0:T(8,128)(2,1)} %param.32) | copy-start | bytes 86404
  12.5 17.1 %copy-start.13 = (bf16[1,2,5,320]{3,1,2,0:T(2,128)(2,1)S(1)}, bf16[1,2,5,320]{3,1,2,0:T(2,128)(2,1)}, u32[]{:S(2)}) copy-start(bf16[1,2,5,320]{3,1,2,0:T(2,128)(2,1)} %param.33) | copy-start | bytes 19204
  12.5 191.6 %all-to-all-start = ((bf16[64,1,2,45,320]{4,2,3,1,0:T(2,128)(2,1)}), bf16[64,1,2,45,320]{4,2,3,1,0:T(2,128)(2,1)}, u32[]{:S(2)}, u32[]{:S(2)}) async-start(bf16[64,1,2,45,320]{4,2,3,1,0:T(2,128)(2,1)} %stack.28), calls=%async_computation | async-start | bytes 8847360 | tf_op jit(solution)/shard_map/all_to_all | solution.py:8
  28.7 167.1 %copy-start = (bf16[2,4,16,320]{3,2,1,0:T(8,128)(2,1)S(1)}, bf16[2,4,16,320]{3,2,1,0:T(8,128)(2,1)}, u32[]{:S(2)}) copy-start(bf16[2,4,16,320]{3,2,1,0:T(8,128)(2,1)} %param.27) | copy-start | bytes 245764
  28.7 167.1 %copy-start.5 = (bf16[2,4,16,320]{3,2,1,0:T(8,128)(2,1)S(1)}, bf16[2,4,16,320]{3,2,1,0:T(8,128)(2,1)}, u32[]{:S(2)}) copy-start(bf16[2,4,16,320]{3,2,1,0:T(8,128)(2,1)} %param.29) | copy-start | bytes 245764
  28.7 167.1 %copy-start.8 = (bf16[2,4,16,320]{3,2,1,0:T(8,128)(2,1)S(1)}, bf16[2,4,16,320]{3,2,1,0:T(8,128)(2,1)}, u32[]{:S(2)}) copy-start(bf16[2,4,16,320]{3,2,1,0:T(8,128)(2,1)} %param.28) | copy-start | bytes 245764
  28.7 196.0 %all-gather.2.cloned.1.call-start = ((), (), s32[]{:S(2)}) async-start(), calls=%async_computation.1 | async-start | bytes 4492800 | tf_op jit(solution)/shard_map/all_gather | solution.py:87
  29.5 565.4 %all-reduce.6.cloned.1.call-start = ((), (), s32[]{:S(2)}) async-start(), calls=%async_computation.2 | async-start | bytes 8192000
  195.9 2.8 collective-permute-start
  197.4 5.2 collective-permute-start.1
  218.8 8.5 %collective-permute-start.3 = (bf16[2,1,16,320]{3,2,1,0:T(8,128)(2,1)}, bf16[2,1,16,320]{3,2,1,0:T(8,128)(2,1)}, u32[]{:S(2)}, u32[]{:S(2)}) collective-permute-start(bf16[2,1,16,320]{3,2,1,0:T(8,128)(2,1)} %get-tuple-element.309), channel_id=1, source_target_pairs={{1,0},{2,1},{3,2},{5,4},{6,5},{7,6},{9,8},{10,9},{11,10},{13,12},{... | collective-permute-start | bytes 61448 | tf_op jit(solution)/shard_map/ppermute | solution.py:23
  220.1 7.3 %collective-permute-start.2 = (bf16[2,1,16,320]{3,2,1,0:T(8,128)(2,1)}, bf16[2,1,16,320]{3,2,1,0:T(8,128)(2,1)}, u32[]{:S(2)}, u32[]{:S(2)}) collective-permute-start(bf16[2,1,16,320]{3,2,1,0:T(8,128)(2,1)} %get-tuple-element.308), channel_id=1, source_target_pairs={{0,1},{1,2},{2,3},{4,5},{5,6},{6,7},{8,9},{9,10},{10,11},{12,13},{... | collective-permute-start | bytes 61448 | tf_op jit(solution)/shard_map/ppermute | solution.py:20
  229.7 18.3 %copy-start.6 = (bf16[2,4,16,320]{3,2,1,0:T(8,128)(2,1)S(1)}, bf16[2,4,16,320]{3,2,1,0:T(8,128)(2,1)}, u32[]{:S(2)}) copy-start(bf16[2,4,16,320]{3,2,1,0:T(8,128)(2,1)} %param.29) | copy-start | bytes 245764
  230.5 17.5 %collective-permute-start.4 = (bf16[2,2,4,16,320]{4,3,2,1,0:T(8,128)(2,1)S(1)}, bf16[2,2,4,16,320]{4,3,2,1,0:T(8,128)(2,1)}, u32[]{:S(2)}, u32[]{:S(2)}) collective-permute-start(bf16[2,2,4,16,320]{4,3,2,1,0:T(8,128)(2,1)S(1)} %get-tuple-element.142), channel_id=1, source_target_pairs={{0,256},{1,257},{2,258},{3,259},{4,260},{5,261},{6,262},{7,263},{8... | collective-permute-start | bytes 491528 | tf_op jit(solution)/shard_map/ppermute | solution.py:31
  249.0 7.5 %copy-start.4 = (bf16[1,1,2880,320]{3,2,1,0:T(8,128)(2,1)S(1)}, bf16[1,1,2880,320]{3,2,1,0:T(8,128)(2,1)}, u32[]{:S(2)}) copy-start(bf16[1,1,2880,320]{3,2,1,0:T(8,128)(2,1)} %copy-done.3) | copy-start | bytes 5529604
  249.0 5.4 collective-permute-start.6
  250.4 5.2 collective-permute-start.5
  260.7 5.6 collective-permute-start.8
  262.0 5.2 collective-permute-start.7
  269.5 5.6 collective-permute-start.10
  270.8 5.2 collective-permute-start.9
  278.2 5.3 collective-permute-start.11
  283.5 6.1 %collective-permute-start.13 = (bf16[2,1,16,320]{3,2,1,0:T(8,128)(2,1)S(1)}, bf16[2,1,16,320]{3,2,1,0:T(8,128)(2,1)S(1)}, u32[]{:S(2)}, u32[]{:S(2)}) collective-permute-start(bf16[2,1,16,320]{3,2,1,0:T(8,128)(2,1)S(1)} %get-tuple-element.303), channel_id=1, source_target_pairs={{1,0},{2,1},{3,2},{5,4},{6,5},{7,6},{9,8},{10,9},{11,10},{13,12},{... | collective-permute-start | bytes 61448 | tf_op jit(solution)/shard_map/ppermute | solution.py:23
  284.8 5.5 collective-permute-start.12
  (9 other events, 15.9 us)
Sparse Core Ops, SparseCore 0:
  32.6 179.1 all-gather.1
  301.6 293.2 all-reduce.5
